TPU v7x, 256 devices: a whole 4x4x8 slice. The times are simulated.
256 devices in a mesh: rep: 16 (over y, z_lo), fsdp: 16 (over z_hi, x, core).
Axes of the slice: x: 4, y: 4, z: 8 (z_hi: 2, z_lo: 4; z = z_hi * 4 + z_lo), core: 2. Of those that a mesh axis runs over, the one named last changes fastest.
Arguments:
- hidden_in: bfloat16 [16, 16, 256, 4096], P('rep', 'fsdp'), may hold values from -6 to 6
- scan_in: bfloat16 [16, 16, 256, 4096], P('rep', 'fsdp'), may hold values from -6 to 6
- grad_out: bfloat16 [16, 16, 256, 4096], P('rep', 'fsdp'), may hold values from -6 to 6
- episodes: int32 [16, 16, 256], P('rep', 'fsdp'), may hold values from 0 to 2, never falling along the last dimension, each value on 1 to 128 neighbouring positions
- gossip_step: int32 [1], replicated, may hold values from 0 to 63
- state_proj: float32 [16, 4096, 256], P('rep', 'fsdp'), may hold values from -0.01953125 to 0.01953125
- step_proj: float32 [16, 32, 4096], P('rep', None, 'fsdp'), may hold values from -0.09375 to 0.09375
- decay_log: float32 [16, 32], P('rep'), may hold values from -5.5 to -3
- step_bias: float32 [16, 32], P('rep'), may hold values from -1 to 1
Outputs:
- layer_grad: bfloat16 [16, 16, 256, 4096], P('rep', 'fsdp')
- scan_grad: bfloat16 [16, 16, 256, 4096], P('rep', 'fsdp')
- new_state_proj: float32 [16, 4096, 256], P('rep', 'fsdp')
- new_step_proj: float32 [16, 32, 4096], P('rep', None, 'fsdp')
- new_decay_log: float32 [16, 32], P('rep')
- new_step_bias: float32 [16, 32], P('rep')
Inputs may be any that keep to these rules, and one draw needn't show every extreme that they name: `episodes`: within each sequence the episode ids never fall; an episode has at most half of 256 tokens, and one has exactly that many.
All inputs are finite; a program needn't handle non-finite values.
Results may differ from a plain program's by a relative error of at most 0.0058.
The roundings to bfloat16 on the way count: a program that leaves them out, or rounds other values in their place, can miss the bound.
Values may be sent and summed in bfloat16 or wider, within the bound.
A program may use at most 128 MiB of HBM per device.

v0:
```python
import functools

import jax
import jax.numpy as jnp
from jax import lax
from jax.experimental import pallas as pl
from jax.experimental.pallas import tpu as pltpu
from jax.sharding import PartitionSpec as P

MESH = pl.DeviceIdType.MESH
F32 = jnp.float32
BF16 = jnp.bfloat16
HIGH = lax.Precision.HIGHEST
LOG2E = 1.4426950408889634
TINY = 1e-37
CAP = 60.0
RATE = 0.1
EPS = 1e-6
WIDTH = 128
BARRIER_NEAR = True


def nn(a, b, precision=None):
    return lax.dot_general(
        a, b, (((1,), (0,)), ((), ())), precision=precision, preferred_element_type=F32
    )


def nt(a, b, precision=None):
    return lax.dot_general(
        a, b, (((1,), (1,)), ((), ())), precision=precision, preferred_element_type=F32
    )


def split3(value):
    high = value.astype(BF16).astype(F32)
    rest = value - high
    mid = rest.astype(BF16).astype(F32)
    return high, mid, rest - mid


def split2(value):
    high = value.astype(BF16)
    return high, (value - high.astype(F32)).astype(BF16)


def triple(product, a, b):
    ah, al = split2(a)
    bh, bl = split2(b)
    return product(ah, bh) + (product(ah, bl) + product(al, bh))


def exact(product, parts, b):
    high, mid, low = (part.astype(BF16) for part in parts)
    return product(high, b) + (product(mid, b) + product(low, b))


def layer_kernel(
    dims,
    state_ref,
    step_ref,
    ep_ref,
    decay_ref,
    bias_ref,
    hid_hbm,
    val_hbm,
    cot_hbm,
    lay_hbm,
    sgr_hbm,
    nstate_ref,
    nstep_ref,
    ndecay_ref,
    nbias_ref,
    hid,
    val,
    cot,
    wts,
    gmat,
    dwo,
    acc,
    from_core,
    hop1,
    direct,
    hop2,
    from_z,
    part_p,
    part_g,
    part_s,
    mate_sums,
    zsend,
    gsend,
    grad_s,
    zero_sum,
    keep,
    heads_in,
    sums_in,
    final_send,
    head_own_s,
    lay,
    sgr,
    feat,
    logit_s,
    mask_s,
    du_s,
    c2_s,
    scores,
    ds,
    vbuf,
    mbuf,
    mrow,
    mcol,
    fgt,
    fg,
    fgl,
    local_sem,
    ssem,
    rsem,
):
    heads, seqs, chunk, rows, bit = dims
    half = rows // 2
    state2 = 2 * WIDTH
    me = lax.axis_index("fsdp")
    rep = lax.axis_index("rep")
    core = lax.rem(me, 2)
    x_at = lax.rem(lax.div(me, 2), 4)
    z_at = lax.div(me, 8)

    def index_of(z, x, c):
        return z * 8 + lax.rem(x, 4) * 2 + c

    other_z = 1 - z_at
    other_c = 1 - core
    right = {"fsdp": index_of(z_at, x_at + 1, core)}
    left = {"fsdp": index_of(z_at, x_at + 3, core)}
    across = {"fsdp": index_of(other_z, x_at, core)}
    twin = {"fsdp": index_of(z_at, x_at, other_c)}
    ahead = 1 + 2 * core
    behind = 3 - 2 * core
    fwd = {"fsdp": index_of(z_at, x_at + ahead, core)}
    back = {"fsdp": index_of(z_at, x_at + behind, core)}
    opposite = {"fsdp": index_of(z_at, x_at + 2, core)}
    peers = [{"fsdp": lax.rem(me + k, seqs)} for k in range(1, seqs)]
    gap = 1 << bit
    mate = {"rep": rep + gap * (1 - 2 * lax.rem(lax.div(rep, gap), 2))}

    used = [0]
    started = []

    def remote(src, dst, number, device):
        return pltpu.make_async_remote_copy(
            src_ref=src,
            dst_ref=dst,
            send_sem=ssem.at[number],
            recv_sem=rsem.at[number],
            device_id=device,
            device_id_type=MESH,
        )

    def send(src, dst, device):
        number = used[0]
        used[0] += 1
        copy = remote(src, dst, number, device)
        copy.start()
        started.append(copy)
        return number

    def landed(dst, number):
        remote(dst, dst, number, twin).wait_recv()

    barrier = pltpu.get_barrier_semaphore()
    near = (twin, right, left, across, mate) if BARRIER_NEAR else peers + [mate]
    for device in near:
        pl.semaphore_signal(barrier, inc=1, device_id=device, device_id_type=MESH)
    loads = [
        pltpu.make_async_copy(val_hbm, val, local_sem.at[0]),
        pltpu.make_async_copy(cot_hbm, cot, local_sem.at[1]),
        pltpu.make_async_copy(hid_hbm, hid, local_sem.at[2]),
    ]
    for load in loads:
        load.start()

    wts[me, :state2] = state_ref[...].astype(BF16)
    wts[me, state2:] = step_ref[...].astype(BF16)
    at_u = lax.broadcasted_iota(jnp.int32, (chunk, chunk), 0)
    at_t = lax.broadcasted_iota(jnp.int32, (chunk, chunk), 1)
    ep_t = jnp.broadcast_to(ep_ref[...].astype(F32), (chunk, chunk))
    mask_s[...] = jnp.where((at_u <= at_t) & (ep_t.T == ep_t), 1.0, 0.0)
    eye_r = lax.broadcasted_iota(jnp.int32, (heads, heads), 0)
    eye_c = lax.broadcasted_iota(jnp.int32, (heads, heads), 1)

    def column(row_ref):
        spread_row = jnp.broadcast_to(row_ref[...], (heads, heads))
        return jnp.sum(jnp.where(eye_r == eye_c, spread_row, 0.0), axis=1, keepdims=True)

    decay = -jnp.exp(column(decay_ref))
    bias_col = column(bias_ref)
    place_r = lax.broadcasted_iota(jnp.int32, (heads, WIDTH), 0)
    place_c = lax.broadcasted_iota(jnp.int32, (heads, WIDTH), 1)
    place_d = jnp.where(place_c == place_r, 1.0, 0.0)
    place_b = jnp.where(place_c == place_r + heads, 1.0, 0.0)
    head_own_s[...] = nn(jnp.broadcast_to(decay_ref[...], (8, heads)), place_d, HIGH) + nn(
        jnp.broadcast_to(bias_ref[...], (8, heads)), place_b, HIGH
    )
    feat[...] = jnp.zeros_like(feat)
    logit_s[...] = jnp.zeros_like(logit_s)
    ds[...] = jnp.zeros_like(ds)

    def prepare(pair, carry):
        for k in range(2):
            h = pair * 2 + k
            lanes = pl.ds(pl.multiple_of(h * WIDTH, WIDTH), WIDTH)
            xh = val[:, lanes]
            gh = cot[:, lanes]
            first = nt(xh[:WIDTH], gh)
            gmat[h, 0] = first[:, :WIDTH]
            gmat[h, 1] = first[:, WIDTH:]
            gmat[h, 2] = nt(xh[WIDTH:], gh[WIDTH:])
        return carry

    pl.semaphore_wait(barrier, len(near))

    top = pl.ds(0, half)
    low = pl.ds(half, half)

    def pass_on(index, part, device):
        return send(wts.at[index, part], wts.at[index, part], device)

    def share(index):
        return send(wts.at[index], wts.at[index], twin)

    def columns(index):
        return pl.ds(pl.multiple_of(index * chunk, chunk), chunk)

    def feat_part(index):
        tokens = hid[:, columns(index)]
        feat[...] += nn(tokens, wts[index, :state2, :])
        logit_s[:, :heads] += nt(tokens, wts[index, state2:, :])

    def shared(z, dx, number):
        index = index_of(z, x_at + dx, other_c)
        landed(wts.at[index], number)
        feat_part(index)

    halves = (top, low)
    n_across = [pass_on(me, part, across) for part in halves]
    n_rt = pass_on(me, top, right)
    n_ll = pass_on(me, low, left)
    n_rl = pass_on(me, low, right)
    n_lt = pass_on(me, top, left)
    n_own = share(me)
    loads[0].wait()
    loads[1].wait()
    lax.fori_loop(0, heads // 2, prepare, 0)
    loads[2].wait()
    feat_part(me)
    shared(z_at, 0, n_own)

    def spread(z, n_rt, n_rl, n_ll, n_lt):
        at_l = index_of(z, x_at + 3, core)
        at_r = index_of(z, x_at + 1, core)
        landed(wts.at[at_l, top], n_rt)
        f_r = pass_on(at_l, top, right)
        landed(wts.at[at_r, low], n_ll)
        f_l = pass_on(at_r, low, left)
        landed(wts.at[at_l, low], n_rl)
        t_l = share(at_l)
        landed(wts.at[at_r, top], n_lt)
        t_r = share(at_r)
        return at_l, at_r, f_r, f_l, t_l, t_r

    at_l, at_r, f_r, f_l, t_l, t_r = spread(z_at, n_rt, n_rl, n_ll, n_lt)
    at_z = index_of(other_z, x_at, core)
    landed(wts.at[at_z, top], n_across[0])
    z_f = pass_on(at_z, top, fwd)
    z_b = pass_on(at_z, top, back)
    landed(wts.at[at_z, low], n_across[1])
    z_2 = pass_on(at_z, low, opposite)
    l_f = pass_on(at_z, low, fwd)
    l_b = pass_on(at_z, low, back)
    t_z = share(at_z)
    feat_part(at_l)
    feat_part(at_r)
    at_2 = index_of(z_at, x_at + 2, core)
    landed(wts.at[at_2, top], f_r)
    landed(wts.at[at_2, low], f_l)
    t_2 = share(at_2)
    feat_part(at_z)
    feat_part(at_2)
    shared(z_at, 3, t_l)
    shared(z_at, 1, t_r)
    far_b = index_of(other_z, x_at + behind, core)
    far_f = index_of(other_z, x_at + ahead, core)
    far_2 = index_of(other_z, x_at + 2, core)
    landed(wts.at[far_b, top], z_f)
    relay = pass_on(far_b, top, fwd)
    shared(other_z, 0, t_z)
    shared(z_at, 2, t_2)
    landed(wts.at[far_f, top], z_b)
    landed(wts.at[far_b, low], l_f)
    t_b = share(far_b)
    landed(wts.at[far_f, low], l_b)
    t_f = share(far_f)
    feat_part(far_b)
    feat_part(far_f)
    landed(wts.at[far_2, low], z_2)
    t_2l = pass_on(far_2, low, twin)
    landed(wts.at[far_2, top], relay)
    t_2t = pass_on(far_2, top, twin)
    feat_part(far_2)
    shared(other_z, ahead, t_b)
    shared(other_z, behind, t_f)
    twin_2 = index_of(other_z, x_at + 2, other_c)
    landed(wts.at[twin_2, low], t_2l)
    landed(wts.at[twin_2, top], t_2t)
    feat_part(twin_2)

    n_part_p = send(wts.at[me], part_p, mate)

    logits = logit_s[...].T[:heads] + bias_col
    small = jnp.exp(-jnp.abs(logits))
    log_part = jnp.where(
        small < 0.01, small * (1.0 - small * (0.5 - small * (1.0 / 3.0))), jnp.log(1.0 + small)
    )
    step = jnp.maximum(logits, 0.0) + log_part
    gate = jnp.where(logits >= 0.0, 1.0, small) / (1.0 + small)
    step_safe = jnp.maximum(step, TINY)
    ratio = jnp.where(logits < -20.0, 1.0, gate / step_safe)
    upper = jnp.where(at_u <= at_t, 1.0, 0.0).astype(BF16)
    c2 = exact(nn, split3(decay * step), upper) * LOG2E
    du = jnp.log2(step_safe) - c2
    du_s[...] = jnp.concatenate([du, jnp.zeros((WIDTH - heads, chunk), F32)], axis=0).T
    c2_s[:, 0, :] = c2
    b_proj = feat[:, :WIDTH]
    c_proj = feat[:, WIDTH:]
    masked = jnp.where(mask_s[...] > 0.5, triple(nt, b_proj, c_proj), 0.0)
    scores[0] = masked[:WIDTH, :WIDTH]
    scores[1] = masked[:WIDTH, WIDTH:]
    scores[2] = masked[WIDTH:, WIDTH:]
    ones8 = jnp.ones((8, chunk), BF16)

    def weigh(h, lane, slot):
        row = c2_s[h, 0:1, :]
        first = jnp.broadcast_to(du_s[:WIDTH, lane : lane + 1], (WIDTH, WIDTH))
        second = jnp.broadcast_to(du_s[WIDTH:, lane : lane + 1], (WIDTH, WIDTH))
        args = (
            jnp.minimum(first + row[:, :WIDTH], CAP),
            first + row[:, WIDTH:],
            jnp.minimum(second + row[:, WIDTH:], CAP),
        )
        for k in range(3):
            e = jnp.exp2(args[k])
            p = gmat[h, k] * e
            ds[k] += p
            vbuf[slot, k] = (e * scores[k]).astype(BF16)
            mbuf[slot, k] = (p * scores[k]).astype(BF16)

    def apply(h, slot):
        lanes = pl.ds(pl.multiple_of(h * WIDTH, WIDTH), WIDTH)
        gh = cot[:, lanes]
        v0 = jnp.concatenate([vbuf[slot, 0], vbuf[slot, 1]], axis=1)
        sgr[:WIDTH, lanes] = nn(v0, gh).astype(BF16)
        sgr[WIDTH:, lanes] = nn(vbuf[slot, 2], gh[WIDTH:]).astype(BF16)
        m0 = jnp.concatenate([mbuf[slot, 0], mbuf[slot, 1]], axis=1)
        m1 = jnp.concatenate([mbuf[slot, 1], mbuf[slot, 2]], axis=0)
        mrow[h, :, :WIDTH] = nn(ones8[:, :WIDTH], mbuf[slot, 0])
        mrow[h, :, WIDTH:] = nn(ones8, m1)
        mcol[h, :, :WIDTH] = nt(ones8, m0)
        mcol[h, :, WIDTH:] = nt(ones8[:, :WIDTH], mbuf[slot, 2])

    weigh(0, 0, 0)

    def head_pair(pair, carry):
        h = pair * 2
        weigh(h + 1, 1, 1)
        apply(h, 0)
        weigh(h + 2, 2, 0)
        apply(h + 1, 1)
        du_s[...] = pltpu.roll(du_s[...], WIDTH - 2, 1)
        return carry

    lax.fori_loop(0, heads // 2 - 1, head_pair, 0)
    weigh(heads - 1, 1, 1)
    apply(heads - 2, 0)
    apply(heads - 1, 1)
    out_sgr = pltpu.make_async_copy(sgr, sgr_hbm, local_sem.at[4])
    out_sgr.start()

    lower = jnp.where(at_u >= at_t, 1.0, 0.0).astype(BF16)
    mc = jnp.sum(mcol[...], axis=1) * 0.125
    drate = exact(nn, split3(jnp.sum(mrow[...], axis=1) * 0.125 - mc), lower)
    dlogit = mc * ratio + gate * (decay * drate)
    ddecay = decay * step * drate
    stack = jnp.concatenate(
        [ddecay, dlogit, jnp.zeros((WIDTH - 2 * heads, chunk), F32)], axis=0
    )
    ds_full = jnp.concatenate(
        [
            jnp.concatenate([ds[0], ds[1]], axis=1),
            jnp.concatenate([jnp.zeros((WIDTH, WIDTH), F32), ds[2]], axis=1),
        ],
        axis=0,
    )
    ds_full = jnp.where(mask_s[...] > 0.5, ds_full, 0.0)
    db = triple(nn, ds_full, c_proj)
    dct = triple(nn, b_proj.T, ds_full)
    fgt[:WIDTH] = db.T.astype(BF16)
    fgt[WIDTH:state2] = dct.astype(BF16)
    fgt[state2:] = dlogit.astype(BF16)

    places = [(z, dx) for z in (other_z, z_at) for dx in (2, ahead, behind, 0)]
    twin_places = [(z, dx) for z in (other_z, z_at) for dx in (2, behind, ahead, 0)]
    n_core = {}

    def twin_part(slot):
        z, dx = twin_places[slot]
        index = index_of(z, x_at + dx, other_c)
        dwo[slot] = nn(fgt[...], hid[:, columns(index)]).astype(BF16)
        n_core[slot] = send(dwo.at[slot], from_core.at[slot], twin)

    def own_part(slot):
        z, dx = places[slot]
        index = index_of(z, x_at + dx, core)
        total = nn(fgt[...], hid[:, columns(index)])
        landed(from_core.at[slot], n_core[slot])
        return total + from_core[slot].astype(F32)

    def layer_part(index):
        spot = columns(index)
        w = wts[index]
        lay[:, spot] = (
            nt(fg[...], w[:state2]) + nn(fgl[:, :heads], w[state2:])
        ).astype(BF16)

    def ring_first(base, k):
        twin_part(base)
        twin_part(base + 1)
        acc[base] = own_part(base).astype(BF16)
        straight = send(acc.at[base, top], direct.at[k], opposite)
        hop = send(acc.at[base, low], hop1.at[k], fwd)
        twin_part(base + 2)
        plus = own_part(base + 1)
        acc[base + 1, top] = plus[:half].astype(BF16)
        keep[k] = plus[half:]
        f_t = send(acc.at[base + 1, top], hop2.at[k, 0, top], fwd)
        twin_part(base + 3)
        acc[base + 2] = own_part(base + 2).astype(BF16)
        b_t = send(acc.at[base + 2, top], hop2.at[k, 1, top], back)
        b_l = send(acc.at[base + 2, low], hop2.at[k, 1, low], back)
        zero_sum[k] = own_part(base + 3)
        return straight, hop, f_t, b_t, b_l

    def ring_next(base, k, hop):
        landed(hop1.at[k], hop)
        acc[base + 1, low] = (keep[k] + hop1[k].astype(F32)).astype(BF16)
        return send(acc.at[base + 1, low], hop2.at[k, 0, low], fwd)

    def ring_end(k, part, from_back, from_fwd):
        landed(hop2.at[k, 0, part], from_back)
        landed(hop2.at[k, 1, part], from_fwd)
        return (
            zero_sum[k, part, :]
            + hop2[k, 0, part, :].astype(F32)
            + hop2[k, 1, part, :].astype(F32)
        )

    def ring_top(k, straight, from_back, from_fwd):
        landed(direct.at[k], straight)
        return ring_end(k, top, from_back, from_fwd) + direct[k].astype(F32)

    straight, hop, f_t, b_t, b_l = ring_first(0, 0)
    f_l = ring_next(0, 0, hop)
    straight2, hop, f_t2, b_t2, b_l2 = ring_first(4, 1)
    zsend[top, :] = ring_top(0, straight, f_t, b_t).astype(BF16)
    n_z = [send(zsend.at[top], from_z.at[top], across)]
    zsend[low, :] = ring_end(0, low, f_l, b_l).astype(BF16)
    n_z.append(send(zsend.at[low], from_z.at[low], across))
    f_l2 = ring_next(4, 1, hop)

    sums8 = exact(lambda a, b: nt(b, a), split3(stack), jnp.ones((8, chunk), BF16))
    heads_in[me] = sums8
    n_heads = [send(heads_in.at[me], heads_in.at[me], device) for device in peers]
    fg[:, :WIDTH] = db.astype(BF16)
    fg[:, WIDTH:] = dct.T.astype(BF16)
    wide = jnp.concatenate([dlogit, jnp.zeros((WIDTH - heads, chunk), F32)], axis=0)
    fgl[...] = wide.T.astype(BF16)
    for index in range(seqs):
        layer_part(index)
    out_lay = pltpu.make_async_copy(lay, lay_hbm, local_sem.at[5])
    out_lay.start()

    for k, number in enumerate(n_heads):
        landed(heads_in.at[lax.rem(me + seqs - k - 1, seqs)], number)
    head_grad = jnp.sum(heads_in[...], axis=0)[:1]
    head_own = head_own_s[:1]
    head_sq = jnp.sum(head_own * head_own, axis=1, keepdims=True) / (2 * heads)
    hgrad_sq = jnp.sum(head_grad * head_grad, axis=1, keepdims=True) / (2 * heads)
    head_trust = jnp.sqrt(head_sq) / jnp.sqrt(hgrad_sq + EPS)
    final_send[...] = jnp.broadcast_to(head_own - RATE * head_trust * head_grad, (8, WIDTH))
    n_final = send(final_send, part_s, mate)
    landed(part_p, n_part_p)

    def lanes_sum(value):
        total = jnp.sum(value * value, axis=0, keepdims=True)
        return total[:, :WIDTH] + total[:, WIDTH:]

    state_own = state_ref[...]
    step_own = step_ref[...]
    own_sq = [lanes_sum(state_own), lanes_sum(step_own)]
    mate_p = part_p[...].astype(F32)
    nstate_ref[...] = 0.5 * (state_own + mate_p[:state2])
    nstep_ref[...] = 0.5 * (step_own + mate_p[state2:])

    n_part_g = {}
    for q in range(2):
        spot = halves[q]
        if q:
            total = ring_end(1, low, f_l2, b_l2)
        else:
            total = ring_top(1, straight2, f_t2, b_t2)
        landed(from_z.at[spot], n_z[q])
        total = total + from_z[spot, :].astype(F32)
        grad_s[spot, :] = total
        gsend[spot, :] = total.astype(BF16)
        n_part_g[q] = send(gsend.at[spot], part_g.at[spot], mate)
    grad = grad_s[...]

    sums_in[me] = jnp.concatenate(
        [lanes_sum(grad[:state2]), lanes_sum(grad[state2:])]
        + own_sq
        + [jnp.zeros((4, WIDTH), F32)],
        axis=0,
    )
    n_sums = [send(sums_in.at[me], sums_in.at[me], device) for device in peers]
    n_mate = [
        send(sums_in.at[me], mate_sums.at[me], dict(mate, fsdp=lax.rem(me + k, seqs)))
        for k in range(seqs)
    ]
    grad_state = grad[:state2].T
    for q in range(2):
        landed(part_g.at[halves[q]], n_part_g[q])
    mate_g = part_g[...].astype(F32)
    mate_state = mate_g[:state2].T
    landed(part_s, n_final)
    head_mix = 0.5 * (final_send[:1] + part_s[:1])
    ndecay_ref[...] = head_mix[:, :heads]
    nbias_ref[...] = head_mix[:, heads : 2 * heads]
    for k, number in enumerate(n_sums):
        landed(sums_in.at[lax.rem(me + seqs - k - 1, seqs)], number)
    for k, number in enumerate(n_mate):
        landed(mate_sums.at[lax.rem(me + seqs - k, seqs)], number)
    width = seqs * chunk

    def trusts(ref):
        squares = jnp.sum(jnp.sum(ref[...], axis=0), axis=1, keepdims=True)
        state_trust = jnp.sqrt(squares[2:3] / (width * state2)) / jnp.sqrt(
            squares[0:1] / (width * state2) + EPS
        )
        step_trust = jnp.sqrt(squares[3:4] / (width * heads)) / jnp.sqrt(
            squares[1:2] / (width * heads) + EPS
        )
        return (0.5 * RATE) * state_trust, (0.5 * RATE) * step_trust

    state_trust, step_trust = trusts(sums_in)
    state_mate, step_mate = trusts(mate_sums)
    nstate_ref[...] -= state_trust * grad_state + state_mate * mate_state
    nstep_ref[...] -= step_trust * grad[state2:] + step_mate * mate_g[state2:]

    out_sgr.wait()
    out_lay.wait()
    for copy in started:
        copy.wait_send()


def place_kernel(*refs):
    count = (len(refs) - 1) // 2
    sem = refs[-1]
    copies = [
        pltpu.make_async_copy(refs[k], refs[count + k], sem.at[k]) for k in range(count)
    ]
    for copy in copies:
        copy.start()
    for copy in copies:
        copy.wait()


def on_device(
    hidden_in, scan_in, grad_out, episodes, gossip_step, state_proj, step_proj, decay_log, step_bias
):
    reps = lax.axis_size("rep")
    seqs = lax.axis_size("fsdp")
    bits = reps.bit_length() - 1
    heads = step_proj.shape[1]
    length, inner = scan_in.shape[2:]
    model = hidden_in.shape[3]
    chunk = model // seqs
    state2 = 2 * WIDTH
    rows = state2 + heads
    half = rows // 2
    vmem = pl.BlockSpec(memory_space=pltpu.VMEM)
    anyspace = pl.BlockSpec(memory_space=pl.ANY)
    copies = 132
    shapes = (
        jax.ShapeDtypeStruct((length, model), BF16),
        jax.ShapeDtypeStruct((length, inner), BF16),
        jax.ShapeDtypeStruct((chunk, state2), F32),
        jax.ShapeDtypeStruct((heads, chunk), F32),
        jax.ShapeDtypeStruct((1, heads), F32),
        jax.ShapeDtypeStruct((1, heads), F32),
    )

    def run(bit, *operands):
        outs = pl.pallas_call(
            functools.partial(layer_kernel, (heads, seqs, chunk, rows, bit)),
            out_shape=shapes,
            in_specs=[vmem] * 5 + [anyspace] * 3,
            out_specs=(anyspace, anyspace, vmem, vmem, vmem, vmem),
            scratch_shapes=[
                pltpu.VMEM((length, model), BF16),
                pltpu.VMEM((length, inner), BF16),
                pltpu.VMEM((length, inner), BF16),
                pltpu.VMEM((seqs, rows, chunk), BF16),
                pltpu.VMEM((heads, 3, WIDTH, WIDTH), F32),
                pltpu.VMEM((8, rows, chunk), BF16),
                pltpu.VMEM((8, rows, chunk), BF16),
                pltpu.VMEM((8, rows, chunk), BF16),
                pltpu.VMEM((2, half, chunk), BF16),
                pltpu.VMEM((2, half, chunk), BF16),
                pltpu.VMEM((2, 2, rows, chunk), BF16),
                pltpu.VMEM((rows, chunk), BF16),
                pltpu.VMEM((rows, chunk), BF16),
                pltpu.VMEM((rows, chunk), BF16),
                pltpu.VMEM((8, WIDTH), F32),
                pltpu.VMEM((seqs, 8, WIDTH), F32),
                pltpu.VMEM((rows, chunk), BF16),
                pltpu.VMEM((rows, chunk), BF16),
                pltpu.VMEM((rows, chunk), F32),
                pltpu.VMEM((2, rows, chunk), F32),
                pltpu.VMEM((2, half, chunk), F32),
                pltpu.VMEM((seqs, 8, WIDTH), F32),
                pltpu.VMEM((seqs, 8, WIDTH), F32),
                pltpu.VMEM((8, WIDTH), F32),
                pltpu.VMEM((8, WIDTH), F32),
                pltpu.VMEM((length, model), BF16),
                pltpu.VMEM((length, inner), BF16),
                pltpu.VMEM((length, state2), F32),
                pltpu.VMEM((length, WIDTH), F32),
                pltpu.VMEM((length, length), F32),
                pltpu.VMEM((length, WIDTH), F32),
                pltpu.VMEM((heads, 8, length), F32),
                pltpu.VMEM((3, WIDTH, WIDTH), F32),
                pltpu.VMEM((3, WIDTH, WIDTH), F32),
                pltpu.VMEM((2, 3, WIDTH, WIDTH), BF16),
                pltpu.VMEM((2, 3, WIDTH, WIDTH), BF16),
                pltpu.VMEM((heads, 8, length), F32),
                pltpu.VMEM((heads, 8, length), F32),
                pltpu.VMEM((rows, length), BF16),
                pltpu.VMEM((length, state2), BF16),
                pltpu.VMEM((length, WIDTH), BF16),
                pltpu.SemaphoreType.DMA((6,)),
                pltpu.SemaphoreType.DMA((copies,)),
                pltpu.SemaphoreType.DMA((copies,)),
            ],
            compiler_params=pltpu.CompilerParams(
                collective_id=bit, has_side_effects=True, vmem_limit_bytes=38 * 1024 * 1024
            ),
        )(*operands)
        return tuple(
            pl.pallas_call(
                place_kernel,
                out_shape=shapes,
                in_specs=[anyspace] * len(shapes),
                out_specs=(anyspace,) * len(shapes),
                scratch_shapes=[pltpu.SemaphoreType.DMA((len(shapes),))],
                compiler_params=pltpu.CompilerParams(vmem_limit_bytes=1024 * 1024),
            )(*outs)
        )

    operands = (
        state_proj[0],
        step_proj[0],
        episodes[0],
        decay_log,
        step_bias,
        hidden_in[0, 0],
        scan_in[0, 0],
        grad_out[0, 0],
    )
    outs = lax.switch(
        lax.rem(gossip_step[0], bits), [functools.partial(run, bit) for bit in range(bits)], *operands
    )
    layer_grad, scan_grad, new_state, new_step, new_decay, new_bias = outs
    return (
        layer_grad[None, None],
        scan_grad[None, None],
        new_state[None],
        new_step[None],
        new_decay,
        new_bias,
    )


def solution(mesh):
    in_specs = (
        P("rep", "fsdp", None, None),
        P("rep", "fsdp", None, None),
        P("rep", "fsdp", None, None),
        P("rep", "fsdp", None),
        P(),
        P("rep", "fsdp", None),
        P("rep", None, "fsdp"),
        P("rep", None),
        P("rep", None),
    )
    out_specs = (
        P("rep", "fsdp", None, None),
        P("rep", "fsdp", None, None),
        P("rep", "fsdp", None),
        P("rep", None, "fsdp"),
        P("rep", None),
        P("rep", None),
    )
    return jax.shard_map(
        on_device, mesh=mesh, in_specs=in_specs, out_specs=out_specs, check_vma=False
    )
```

profile of v0, /device:TPU:33, one launch (start us, length us, event | category | flops | bytes accessed | tf_op | source)
XLA Modules:
  0.0 68.7 jit_solution(12966107700779670594)
XLA Ops:
  1.3 67.2 %conditional.1 = ((bf16[256,4096]{1,0:T(8,128)(2,1)}, bf16[256,4096]{1,0:T(8,128)(2,1)}, f32[256,256]{1,0:T(8,128)}, f32[32,256]{1,0:T(8,128)}, f32[1,32]{1,0:T(1,128)}, /*index=5*/f32[1,32]{1,0:T(1,128)})) conditional(s32[]{:T(128)} %clamp.3, (f32[256,256]{1,0:T(8,128)}, f32[32,256]{1,0:T(8,128)}, ...), branch_computations={%region_0.0_spmd.clone, %region_1.0_spmd.clone, %region_2.0_spmd.c... | conditional | bytes 8 | solution.py:688
  1.5 64.2 %branch_2_fun.4 = (bf16[256,4096]{1,0:T(8,128)(2,1)S(1)}, bf16[256,4096]{1,0:T(8,128)(2,1)S(1)}, f32[256,256]{1,0:T(8,128)S(1)}, f32[32,256]{1,0:T(8,128)S(1)}, ...) custom-call(f32[256,256]{1,0:T(8,128)} %get-tuple-element.244.state_ref, f32[32,256]{1,0:T(8,128)} %get-tuple-element.245.step_ref, ...), custom_call_target="tpu_custom_call" | custom-call | tf_op jit(solution)/shard_map/cond/branch_2_fun/pallas_call | solution.py:612
  65.8 2.1 %branch_2_fun.5 = (bf16[256,4096]{1,0:T(8,128)(2,1)}, bf16[256,4096]{1,0:T(8,128)(2,1)}, f32[256,256]{1,0:T(8,128)}, f32[32,256]{1,0:T(8,128)}, f32[1,32]{1,0:T(1,128)}, /*index=5*/f32[1,32]{1,0:T(1,128)}) custom-call(bf16[256,4096]{1,0:T(8,128)(2,1)S(1)} %get-tuple-element.252.refs_0_, bf16[256,4096]{1,0:T(8,128)(2,1)S(1)} %get-tuple-element.253.refs_1_, ...), custom_call_target="tpu_custom_call" | custom-call | tf_op jit(solution)/shard_map/cond/branch_2_fun/pallas_call | solution.py:668
where the time goes:
time: 68.8 us; the launch traced here: 68.7 us
  Pallas kernels  66.4 us (97%)
  between operations  1.51 us (2%)
  loops' own time  0.82 us (1%)
    pallas_call x1, Pallas kernels, run(): pl.pallas_call(functools.partial(layer_kernel, (heads, seqs, chunk, rows,...  64.2 us
    pallas_call x1, Pallas kernels, run(): pl.pallas_call(place_kernel, out_shape=shapes, in_specs=[anyspace] * len(...  2.14 us

commit v1 on v0

--- a/solution.py
+++ b/solution.py
@@ -18,6 +18,7 @@
 EPS = 1e-6
 WIDTH = 128
 BARRIER_NEAR = True
+EARLY = 10
 
 
 def nn(a, b, precision=None):
@@ -65,8 +66,8 @@
     hid_hbm,
     val_hbm,
     cot_hbm,
-    lay_hbm,
-    sgr_hbm,
+    lay,
+    sgr,
     nstate_ref,
     nstep_ref,
     ndecay_ref,
@@ -96,8 +97,6 @@
     sums_in,
     final_send,
     head_own_s,
-    lay,
-    sgr,
     feat,
     logit_s,
     mask_s,
@@ -271,12 +270,12 @@
     at_l, at_r, f_r, f_l, t_l, t_r = spread(z_at, n_rt, n_rl, n_ll, n_lt)
     at_z = index_of(other_z, x_at, core)
     landed(wts.at[at_z, top], n_across[0])
-    z_f = pass_on(at_z, top, fwd)
-    z_b = pass_on(at_z, top, back)
+    def scatter(part):
+        return [pass_on(at_z, part, device) for device in (opposite, fwd, back)]
+
+    far = [scatter(top)]
     landed(wts.at[at_z, low], n_across[1])
-    z_2 = pass_on(at_z, low, opposite)
-    l_f = pass_on(at_z, low, fwd)
-    l_b = pass_on(at_z, low, back)
+    far.append(scatter(low))
     t_z = share(at_z)
     feat_part(at_l)
     feat_part(at_r)
@@ -291,28 +290,25 @@
     far_b = index_of(other_z, x_at + behind, core)
     far_f = index_of(other_z, x_at + ahead, core)
     far_2 = index_of(other_z, x_at + 2, core)
-    landed(wts.at[far_b, top], z_f)
-    relay = pass_on(far_b, top, fwd)
+    far_own = (far_2, far_b, far_f)
+    far_twin = (
+        index_of(other_z, x_at + 2, other_c),
+        index_of(other_z, x_at + ahead, other_c),
+        index_of(other_z, x_at + behind, other_c),
+    )
     shared(other_z, 0, t_z)
     shared(z_at, 2, t_2)
-    landed(wts.at[far_f, top], z_b)
-    landed(wts.at[far_b, low], l_f)
-    t_b = share(far_b)
-    landed(wts.at[far_f, low], l_b)
-    t_f = share(far_f)
-    feat_part(far_b)
-    feat_part(far_f)
-    landed(wts.at[far_2, low], z_2)
-    t_2l = pass_on(far_2, low, twin)
-    landed(wts.at[far_2, top], relay)
-    t_2t = pass_on(far_2, top, twin)
-    feat_part(far_2)
-    shared(other_z, ahead, t_b)
-    shared(other_z, behind, t_f)
-    twin_2 = index_of(other_z, x_at + 2, other_c)
-    landed(wts.at[twin_2, low], t_2l)
-    landed(wts.at[twin_2, top], t_2t)
-    feat_part(twin_2)
+    t_far = {}
+    for p, part in enumerate(halves):
+        for k in (1, 2, 0):
+            landed(wts.at[far_own[k], part], far[p][k])
+            t_far[p, k] = pass_on(far_own[k], part, twin)
+    for k in (1, 2, 0):
+        feat_part(far_own[k])
+    for k in (1, 2, 0):
+        for p, part in enumerate(halves):
+            landed(wts.at[far_twin[k], part], t_far[p, k])
+        feat_part(far_twin[k])
 
     n_part_p = send(wts.at[me], part_p, mate)
 
@@ -382,8 +378,6 @@
     weigh(heads - 1, 1, 1)
     apply(heads - 2, 0)
     apply(heads - 1, 1)
-    out_sgr = pltpu.make_async_copy(sgr, sgr_hbm, local_sem.at[4])
-    out_sgr.start()
 
     lower = jnp.where(at_u >= at_t, 1.0, 0.0).astype(BF16)
     mc = jnp.sum(mcol[...], axis=1) * 0.125
@@ -435,7 +429,7 @@
         twin_part(base)
         twin_part(base + 1)
         acc[base] = own_part(base).astype(BF16)
-        straight = send(acc.at[base, top], direct.at[k], opposite)
+        straight = send(acc.at[base, top], direct.at[k, top], opposite)
         hop = send(acc.at[base, low], hop1.at[k], fwd)
         twin_part(base + 2)
         plus = own_part(base + 1)
@@ -464,29 +458,54 @@
         )
 
     def ring_top(k, straight, from_back, from_fwd):
-        landed(direct.at[k], straight)
-        return ring_end(k, top, from_back, from_fwd) + direct[k].astype(F32)
-
-    straight, hop, f_t, b_t, b_l = ring_first(0, 0)
-    f_l = ring_next(0, 0, hop)
+        landed(direct.at[k, top], straight)
+        return ring_end(k, top, from_back, from_fwd) + direct[k, top, :].astype(F32)
+
+    twin_part(0)
+    twin_part(1)
+    acc[0] = own_part(0).astype(BF16)
+    ways = ((0, direct.at[0], opposite), (1, hop2.at[0, 0], fwd), (2, hop2.at[0, 1], back))
+    far = {}
+
+    def straight_send(k, p):
+        slot, into, device = ways[k]
+        far[k, p] = send(acc.at[slot, halves[p]], into.at[halves[p]], device)
+
+    straight_send(0, 0)
+    twin_part(2)
+    acc[1] = own_part(1).astype(BF16)
+    straight_send(1, 0)
+    twin_part(3)
+    acc[2] = own_part(2).astype(BF16)
+    straight_send(2, 0)
+    for k in range(3):
+        straight_send(k, 1)
+    zero_sum[0] = own_part(3)
     straight2, hop, f_t2, b_t2, b_l2 = ring_first(4, 1)
-    zsend[top, :] = ring_top(0, straight, f_t, b_t).astype(BF16)
-    n_z = [send(zsend.at[top], from_z.at[top], across)]
-    zsend[low, :] = ring_end(0, low, f_l, b_l).astype(BF16)
-    n_z.append(send(zsend.at[low], from_z.at[low], across))
-    f_l2 = ring_next(4, 1, hop)
-
-    sums8 = exact(lambda a, b: nt(b, a), split3(stack), jnp.ones((8, chunk), BF16))
-    heads_in[me] = sums8
-    n_heads = [send(heads_in.at[me], heads_in.at[me], device) for device in peers]
     fg[:, :WIDTH] = db.astype(BF16)
     fg[:, WIDTH:] = dct.T.astype(BF16)
     wide = jnp.concatenate([dlogit, jnp.zeros((WIDTH - heads, chunk), F32)], axis=0)
     fgl[...] = wide.T.astype(BF16)
-    for index in range(seqs):
+    for index in range(EARLY):
         layer_part(index)
-    out_lay = pltpu.make_async_copy(lay, lay_hbm, local_sem.at[5])
-    out_lay.start()
+    n_z = []
+    for p, part in enumerate(halves):
+        for k in range(3):
+            landed(ways[k][1].at[part], far[k, p])
+        zsend[part, :] = (
+            zero_sum[0, part, :]
+            + direct[0, part, :].astype(F32)
+            + hop2[0, 0, part, :].astype(F32)
+            + hop2[0, 1, part, :].astype(F32)
+        ).astype(BF16)
+        n_z.append(send(zsend.at[part], from_z.at[part], across))
+    f_l2 = ring_next(4, 1, hop)
+
+    sums8 = exact(lambda a, b: nt(b, a), split3(stack), jnp.ones((8, chunk), BF16))
+    heads_in[me] = sums8
+    n_heads = [send(heads_in.at[me], heads_in.at[me], device) for device in peers]
+    for index in range(EARLY, seqs):
+        layer_part(index)
 
     for k, number in enumerate(n_heads):
         landed(heads_in.at[lax.rem(me + seqs - k - 1, seqs)], number)
@@ -565,8 +584,6 @@
     nstate_ref[...] -= state_trust * grad_state + state_mate * mate_state
     nstep_ref[...] -= step_trust * grad[state2:] + step_mate * mate_g[state2:]
 
-    out_sgr.wait()
-    out_lay.wait()
     for copy in started:
         copy.wait_send()
 
@@ -613,7 +630,7 @@
             functools.partial(layer_kernel, (heads, seqs, chunk, rows, bit)),
             out_shape=shapes,
             in_specs=[vmem] * 5 + [anyspace] * 3,
-            out_specs=(anyspace, anyspace, vmem, vmem, vmem, vmem),
+            out_specs=(vmem,) * len(shapes),
             scratch_shapes=[
                 pltpu.VMEM((length, model), BF16),
                 pltpu.VMEM((length, inner), BF16),
@@ -624,7 +641,7 @@
                 pltpu.VMEM((8, rows, chunk), BF16),
                 pltpu.VMEM((8, rows, chunk), BF16),
                 pltpu.VMEM((2, half, chunk), BF16),
-                pltpu.VMEM((2, half, chunk), BF16),
+                pltpu.VMEM((2, rows, chunk), BF16),
                 pltpu.VMEM((2, 2, rows, chunk), BF16),
                 pltpu.VMEM((rows, chunk), BF16),
                 pltpu.VMEM((rows, chunk), BF16),
@@ -640,8 +657,6 @@
                 pltpu.VMEM((seqs, 8, WIDTH), F32),
                 pltpu.VMEM((8, WIDTH), F32),
                 pltpu.VMEM((8, WIDTH), F32),
-                pltpu.VMEM((length, model), BF16),
-                pltpu.VMEM((length, inner), BF16),
                 pltpu.VMEM((length, state2), F32),
                 pltpu.VMEM((length, WIDTH), F32),
                 pltpu.VMEM((length, length), F32),
@@ -656,7 +671,7 @@
                 pltpu.VMEM((rows, length), BF16),
                 pltpu.VMEM((length, state2), BF16),
                 pltpu.VMEM((length, WIDTH), BF16),
-                pltpu.SemaphoreType.DMA((6,)),
+                pltpu.SemaphoreType.DMA((3,)),
                 pltpu.SemaphoreType.DMA((copies,)),
                 pltpu.SemaphoreType.DMA((copies,)),
             ],

time: 68.8 us -> 70.4 us (1.023)
  the two profiles are of different devices: /device:TPU:33 before, /device:TPU:1 now
where the time goes in v1:
time: 70.4 us; the launch traced here: 70 us
  Pallas kernels  67.7 us (96%)
  between operations  1.51 us (2%)
  loops' own time  0.82 us (1%)
    pallas_call x1, Pallas kernels, run(): pl.pallas_call(functools.partial(layer_kernel, (heads, seqs, chunk, rows,...  65.5 us
    pallas_call x1, Pallas kernels, run(): pl.pallas_call(place_kernel, out_shape=shapes, in_specs=[anyspace] * len(...  2.14 us

profile of v1, /device:TPU:1, one launch (start us, length us, event | category | flops | bytes accessed | tf_op | source)
XLA Modules:
  0.0 70.0 jit_solution(14086589299650836971)
XLA Ops:
  1.3 68.5 %conditional.1 = ((bf16[256,4096]{1,0:T(8,128)(2,1)}, bf16[256,4096]{1,0:T(8,128)(2,1)}, f32[256,256]{1,0:T(8,128)}, f32[32,256]{1,0:T(8,128)}, f32[1,32]{1,0:T(1,128)}, /*index=5*/f32[1,32]{1,0:T(1,128)})) conditional(s32[]{:T(128)} %clamp.3, (f32[256,256]{1,0:T(8,128)}, f32[32,256]{1,0:T(8,128)}, ...), branch_computations={%region_0.0_spmd.clone, %region_1.0_spmd.clone, %region_2.0_spmd.c... | conditional | bytes 8 | solution.py:703
  1.8 65.5 %branch_3_fun.4 = (bf16[256,4096]{1,0:T(8,128)(2,1)S(1)}, bf16[256,4096]{1,0:T(8,128)(2,1)S(1)}, f32[256,256]{1,0:T(8,128)S(1)}, f32[32,256]{1,0:T(8,128)S(1)}, ...) custom-call(f32[256,256]{1,0:T(8,128)} %get-tuple-element.259.state_ref, f32[32,256]{1,0:T(8,128)} %get-tuple-element.260.step_ref, ...), custom_call_target="tpu_custom_call" | custom-call | tf_op jit(solution)/shard_map/cond/branch_3_fun/pallas_call | solution.py:629
  67.3 2.1 %branch_3_fun.5 = (bf16[256,4096]{1,0:T(8,128)(2,1)}, bf16[256,4096]{1,0:T(8,128)(2,1)}, f32[256,256]{1,0:T(8,128)}, f32[32,256]{1,0:T(8,128)}, f32[1,32]{1,0:T(1,128)}, /*index=5*/f32[1,32]{1,0:T(1,128)}) custom-call(bf16[256,4096]{1,0:T(8,128)(2,1)S(1)} %get-tuple-element.267.refs_0_, bf16[256,4096]{1,0:T(8,128)(2,1)S(1)} %get-tuple-element.268.refs_1_, ...), custom_call_target="tpu_custom_call" | custom-call | tf_op jit(solution)/shard_map/cond/branch_3_fun/pallas_call | solution.py:683

commit v2 on v1

--- a/solution.py
+++ b/solution.py
@@ -58,11 +58,11 @@
 
 def layer_kernel(
     dims,
-    state_ref,
-    step_ref,
-    ep_ref,
-    decay_ref,
-    bias_ref,
+    state_hbm,
+    step_hbm,
+    ep_hbm,
+    decay_hbm,
+    bias_hbm,
     hid_hbm,
     val_hbm,
     cot_hbm,
@@ -72,6 +72,11 @@
     nstep_ref,
     ndecay_ref,
     nbias_ref,
+    state_ref,
+    step_ref,
+    ep_ref,
+    decay_ref,
+    bias_ref,
     hid,
     val,
     cot,
@@ -170,6 +175,20 @@
     near = (twin, right, left, across, mate) if BARRIER_NEAR else peers + [mate]
     for device in near:
         pl.semaphore_signal(barrier, inc=1, device_id=device, device_id_type=MESH)
+    small_loads = [
+        pltpu.make_async_copy(src, dst, local_sem.at[3 + k])
+        for k, (src, dst) in enumerate(
+            (
+                (state_hbm, state_ref),
+                (step_hbm, step_ref),
+                (ep_hbm, ep_ref),
+                (decay_hbm, decay_ref),
+                (bias_hbm, bias_ref),
+            )
+        )
+    ]
+    for load in small_loads:
+        load.start()
     loads = [
         pltpu.make_async_copy(val_hbm, val, local_sem.at[0]),
         pltpu.make_async_copy(cot_hbm, cot, local_sem.at[1]),
@@ -178,6 +197,8 @@
     for load in loads:
         load.start()
 
+    for load in small_loads:
+        load.wait()
     wts[me, :state2] = state_ref[...].astype(BF16)
     wts[me, state2:] = step_ref[...].astype(BF16)
     at_u = lax.broadcasted_iota(jnp.int32, (chunk, chunk), 0)
@@ -482,6 +503,9 @@
         straight_send(k, 1)
     zero_sum[0] = own_part(3)
     straight2, hop, f_t2, b_t2, b_l2 = ring_first(4, 1)
+    sums8 = exact(lambda a, b: nt(b, a), split3(stack), jnp.ones((8, chunk), BF16))
+    heads_in[me] = sums8
+    n_heads = [send(heads_in.at[me], heads_in.at[me], device) for device in peers]
     fg[:, :WIDTH] = db.astype(BF16)
     fg[:, WIDTH:] = dct.T.astype(BF16)
     wide = jnp.concatenate([dlogit, jnp.zeros((WIDTH - heads, chunk), F32)], axis=0)
@@ -501,9 +525,6 @@
         n_z.append(send(zsend.at[part], from_z.at[part], across))
     f_l2 = ring_next(4, 1, hop)
 
-    sums8 = exact(lambda a, b: nt(b, a), split3(stack), jnp.ones((8, chunk), BF16))
-    heads_in[me] = sums8
-    n_heads = [send(heads_in.at[me], heads_in.at[me], device) for device in peers]
     for index in range(EARLY, seqs):
         layer_part(index)
 
@@ -615,7 +636,7 @@
     half = rows // 2
     vmem = pl.BlockSpec(memory_space=pltpu.VMEM)
     anyspace = pl.BlockSpec(memory_space=pl.ANY)
-    copies = 132
+    copies = 97
     shapes = (
         jax.ShapeDtypeStruct((length, model), BF16),
         jax.ShapeDtypeStruct((length, inner), BF16),
@@ -629,9 +650,14 @@
         outs = pl.pallas_call(
             functools.partial(layer_kernel, (heads, seqs, chunk, rows, bit)),
             out_shape=shapes,
-            in_specs=[vmem] * 5 + [anyspace] * 3,
+            in_specs=[anyspace] * 8,
             out_specs=(vmem,) * len(shapes),
             scratch_shapes=[
+                pltpu.VMEM((chunk, state2), F32),
+                pltpu.VMEM((heads, chunk), F32),
+                pltpu.VMEM((1, length), jnp.int32),
+                pltpu.VMEM((1, heads), F32),
+                pltpu.VMEM((1, heads), F32),
                 pltpu.VMEM((length, model), BF16),
                 pltpu.VMEM((length, inner), BF16),
                 pltpu.VMEM((length, inner), BF16),
@@ -671,7 +697,7 @@
                 pltpu.VMEM((rows, length), BF16),
                 pltpu.VMEM((length, state2), BF16),
                 pltpu.VMEM((length, WIDTH), BF16),
-                pltpu.SemaphoreType.DMA((3,)),
+                pltpu.SemaphoreType.DMA((8,)),
                 pltpu.SemaphoreType.DMA((copies,)),
                 pltpu.SemaphoreType.DMA((copies,)),
             ],

time: 70.4 us -> 68.3 us (0.970)
  Pallas kernels: 67.7 us -> 66 us
    pallas_call x1, Pallas kernels: 65.5 us -> 63.8 us  [run(): pl.pallas_call(functools.partial(layer_kernel, (heads, seqs, chunk, rows,...]
where the time goes in v2:
time: 68.3 us; the launch traced here: 68.2 us
  Pallas kernels  66 us (97%)
  between operations  1.51 us (2%)
  loops' own time  0.74 us (1%)
    pallas_call x1, Pallas kernels, run(): pl.pallas_call(functools.partial(layer_kernel, (heads, seqs, chunk, rows,...  63.8 us
    pallas_call x1, Pallas kernels, run(): pl.pallas_call(place_kernel, out_shape=shapes, in_specs=[anyspace] * len(...  2.14 us

profile of v2, /device:TPU:1, one launch (start us, length us, event | category | flops | bytes accessed | tf_op | source)
XLA Modules:
  0.0 68.2 jit_solution(1179791307723850716)
XLA Ops:
  1.3 66.7 %conditional.1 = ((bf16[256,4096]{1,0:T(8,128)(2,1)}, bf16[256,4096]{1,0:T(8,128)(2,1)}, f32[256,256]{1,0:T(8,128)}, f32[32,256]{1,0:T(8,128)}, f32[1,32]{1,0:T(1,128)}, /*index=5*/f32[1,32]{1,0:T(1,128)})) conditional(s32[]{:T(128)} %clamp.3, (f32[256,256]{1,0:T(8,128)}, f32[32,256]{1,0:T(8,128)}, ...), branch_computations={%region_0.0_spmd.clone, %region_1.0_spmd.clone, %region_2.0_spmd.c... | conditional | bytes 8 | solution.py:729
  1.5 63.8 %branch_1_fun.4 = (bf16[256,4096]{1,0:T(8,128)(2,1)S(1)}, bf16[256,4096]{1,0:T(8,128)(2,1)S(1)}, f32[256,256]{1,0:T(8,128)S(1)}, f32[32,256]{1,0:T(8,128)S(1)}, ...) custom-call(f32[256,256]{1,0:T(8,128)} %get-tuple-element.229.state_hbm, f32[32,256]{1,0:T(8,128)} %get-tuple-element.230.step_hbm, ...), custom_call_target="tpu_custom_call" | custom-call | tf_op jit(solution)/shard_map/cond/branch_1_fun/pallas_call | solution.py:650
  65.3 2.1 %branch_1_fun.5 = (bf16[256,4096]{1,0:T(8,128)(2,1)}, bf16[256,4096]{1,0:T(8,128)(2,1)}, f32[256,256]{1,0:T(8,128)}, f32[32,256]{1,0:T(8,128)}, f32[1,32]{1,0:T(1,128)}, /*index=5*/f32[1,32]{1,0:T(1,128)}) custom-call(bf16[256,4096]{1,0:T(8,128)(2,1)S(1)} %get-tuple-element.237.refs_0_, bf16[256,4096]{1,0:T(8,128)(2,1)S(1)} %get-tuple-element.238.refs_1_, ...), custom_call_target="tpu_custom_call" | custom-call | tf_op jit(solution)/shard_map/cond/branch_1_fun/pallas_call | solution.py:709

commit v3 on v2

--- a/solution.py
+++ b/solution.py
@@ -502,7 +502,6 @@
     for k in range(3):
         straight_send(k, 1)
     zero_sum[0] = own_part(3)
-    straight2, hop, f_t2, b_t2, b_l2 = ring_first(4, 1)
     sums8 = exact(lambda a, b: nt(b, a), split3(stack), jnp.ones((8, chunk), BF16))
     heads_in[me] = sums8
     n_heads = [send(heads_in.at[me], heads_in.at[me], device) for device in peers]
@@ -512,6 +511,7 @@
     fgl[...] = wide.T.astype(BF16)
     for index in range(EARLY):
         layer_part(index)
+    straight2, hop, f_t2, b_t2, b_l2 = ring_first(4, 1)
     n_z = []
     for p, part in enumerate(halves):
         for k in range(3):

time: 68.3 us -> 64.4 us (0.943); the launches traced: 68.2 us -> 63.5 us
  Pallas kernels: 66 us -> 61.2 us
    pallas_call x1, Pallas kernels: 63.8 us -> 59 us  [run(): pl.pallas_call(functools.partial(layer_kernel, (heads, seqs, chunk, rows,...]
where the time goes in v3:
time: 64.4 us; the launch traced here: 63.5 us
  Pallas kernels  61.2 us (95%)
  between operations  1.51 us (2%)
  loops' own time  0.82 us (1%)
    pallas_call x1, Pallas kernels, run(): pl.pallas_call(functools.partial(layer_kernel, (heads, seqs, chunk, rows,...  59 us
    pallas_call x1, Pallas kernels, run(): pl.pallas_call(place_kernel, out_shape=shapes, in_specs=[anyspace] * len(...  2.14 us

profile of v3, /device:TPU:1, one launch (start us, length us, event | category | flops | bytes accessed | tf_op | source)
XLA Modules:
  0.0 63.5 jit_solution(14022342449950838741)
XLA Ops:
  1.3 62.0 %conditional.1 = ((bf16[256,4096]{1,0:T(8,128)(2,1)}, bf16[256,4096]{1,0:T(8,128)(2,1)}, f32[256,256]{1,0:T(8,128)}, f32[32,256]{1,0:T(8,128)}, f32[1,32]{1,0:T(1,128)}, /*index=5*/f32[1,32]{1,0:T(1,128)})) conditional(s32[]{:T(128)} %clamp.3, (f32[256,256]{1,0:T(8,128)}, f32[32,256]{1,0:T(8,128)}, ...), branch_computations={%region_0.0_spmd.clone, %region_1.0_spmd.clone, %region_2.0_spmd.c... | conditional | bytes 8 | solution.py:729
  1.5 59.0 %branch_2_fun.4 = (bf16[256,4096]{1,0:T(8,128)(2,1)S(1)}, bf16[256,4096]{1,0:T(8,128)(2,1)S(1)}, f32[256,256]{1,0:T(8,128)S(1)}, f32[32,256]{1,0:T(8,128)S(1)}, ...) custom-call(f32[256,256]{1,0:T(8,128)} %get-tuple-element.244.state_hbm, f32[32,256]{1,0:T(8,128)} %get-tuple-element.245.step_hbm, ...), custom_call_target="tpu_custom_call" | custom-call | tf_op jit(solution)/shard_map/cond/branch_2_fun/pallas_call | solution.py:650
  60.6 2.1 %branch_2_fun.5 = (bf16[256,4096]{1,0:T(8,128)(2,1)}, bf16[256,4096]{1,0:T(8,128)(2,1)}, f32[256,256]{1,0:T(8,128)}, f32[32,256]{1,0:T(8,128)}, f32[1,32]{1,0:T(1,128)}, /*index=5*/f32[1,32]{1,0:T(1,128)}) custom-call(bf16[256,4096]{1,0:T(8,128)(2,1)S(1)} %get-tuple-element.252.refs_0_, bf16[256,4096]{1,0:T(8,128)(2,1)S(1)} %get-tuple-element.253.refs_1_, ...), custom_call_target="tpu_custom_call" | custom-call | tf_op jit(solution)/shard_map/cond/branch_2_fun/pallas_call | solution.py:709
